TPU v7x, 32 devices: a whole 2x2x4 slice. The times are simulated.
32 devices in a mesh: dp: 4 (over z), group: 8 (over y, x, core).
Axes of the slice: x: 2, y: 2, z: 4, core: 2. Of those that a mesh axis runs over, the one named last changes fastest.
Arguments:
- qkv: bfloat16 [2048, 1920], P(('dp', 'group')), may hold values from -200 to 200
- embed_grad: bfloat16 [2048, 1280], P(('dp', 'group')), may hold values from -0.59765625 to 0.59765625
- out_weight: bfloat16 [1280, 640], replicated, may hold values from -0.25 to 0.25
- image_len: int32 [4, 8, 8], P('dp'), may hold values from 0 to 8, as said below
- image_order: int32 [4, 8, 8], P('dp', 'group'), may hold values from 0 to 7, each once within a row
- image_cut: int32 [4, 8], P('dp', 'group'), may hold values from 8 to 24
Outputs:
- embeds: bfloat16 [2048, 1280], P(('dp', 'group'))
- qkv_grad: bfloat16 [2048, 1920], P(('dp', 'group'))
- weight_grad: float32 [1280, 640], P('group')
Inputs may be any that keep to these rules, and one draw needn't show every extreme that they name: For every replica r and destination d, the sum over sources s of image_len[r, s, d] is exactly 32; 0 means that s sends nothing to d. Each image_order[r, s] names every destination once.
All inputs are finite; a program needn't handle non-finite values.
Results may differ from a plain program's by a relative error of at most 0.017.
Values may be sent and summed in bfloat16 or wider, within the bound.
A program may use at most 64 MiB of HBM per device.

v0:
```python
import math

import jax
import jax.numpy as jnp
from jax import lax
from jax.sharding import PartitionSpec as P

HD = 80
HEADS = 8
SLOT = 8


masked_value = -1e30


def attention_pass(qkv_rows, cot_rows, out_weight, allowed, live):
    count = qkv_rows.shape[0]
    head_feats = out_weight.shape[1]
    score_scale = 1.0 / math.sqrt(HD)
    query = qkv_rows[:, :head_feats].reshape(count, HEADS, HD)
    keys = qkv_rows[:, head_feats : 2 * head_feats].reshape(count, HEADS, HD)
    values = qkv_rows[:, 2 * head_feats :].reshape(count, HEADS, HD)
    scores = (
        jnp.einsum("qhe,khe->hqk", query, keys, preferred_element_type=jnp.float32) * score_scale
    )
    scores = jnp.where(allowed[None], scores, masked_value)
    top = jnp.max(scores, axis=-1, keepdims=True)
    expo = jnp.exp(scores - top)
    probs = expo / jnp.sum(expo, axis=-1, keepdims=True)
    probs = jnp.where(live[None, :, None], probs, 0.0)
    probs_b = probs.astype(jnp.bfloat16)
    attended = jnp.einsum(
        "hqk,khe->qhe", probs_b, values, preferred_element_type=jnp.float32
    ).astype(jnp.bfloat16)
    att_rows = attended.reshape(count, head_feats)
    embed_rows = lax.dot_general(
        att_rows, out_weight, (((1,), (1,)), ((), ())), preferred_element_type=jnp.float32
    ).astype(jnp.bfloat16)
    att_grad = jnp.dot(cot_rows, out_weight, preferred_element_type=jnp.float32).astype(
        jnp.bfloat16
    )
    grad_heads = att_grad.reshape(count, HEADS, HD)
    prob_grad = jnp.einsum("qhe,khe->hqk", grad_heads, values, preferred_element_type=jnp.float32)
    delta = jnp.sum(grad_heads.astype(jnp.float32) * attended.astype(jnp.float32), axis=-1)
    delta = jnp.transpose(delta, (1, 0))[:, :, None]
    score_grad = (probs * (prob_grad - delta) * score_scale).astype(jnp.bfloat16)
    query_grad = jnp.einsum(
        "hqk,khe->qhe", score_grad, keys, preferred_element_type=jnp.float32
    ).astype(jnp.bfloat16)
    keys_grad = jnp.einsum(
        "hqk,qhe->khe", score_grad, query, preferred_element_type=jnp.float32
    ).astype(jnp.bfloat16)
    values_grad = jnp.einsum(
        "hqk,qhe->khe", probs_b, grad_heads, preferred_element_type=jnp.float32
    ).astype(jnp.bfloat16)
    grad_rows = jnp.concatenate(
        [
            query_grad.reshape(count, head_feats),
            keys_grad.reshape(count, head_feats),
            values_grad.reshape(count, head_feats),
        ],
        axis=1,
    )
    return (embed_rows, grad_rows, att_rows)


def local(qkv, embed_grad, out_weight, image_len, image_order, image_cut):
    groups = lax.axis_size("group")
    own_index = lax.axis_index("group")
    slot_rows = SLOT
    src_rows = qkv.shape[0]
    width = out_weight.shape[0]
    head_feats = out_weight.shape[1]
    dest_range = jnp.arange(groups, dtype=jnp.int32)
    within = jnp.arange(slot_rows, dtype=jnp.int32)
    lens_all = image_len[0]
    lens_row = lax.dynamic_index_in_dim(lens_all, own_index, 0, keepdims=False)
    order_row = image_order[0, 0]
    onehot = (order_row[:, None] == dest_range[None, :]).astype(jnp.int32)
    ordered = jnp.sum(onehot * lens_row[None, :], axis=1)
    image_ends = jnp.cumsum(ordered)
    image_starts = image_ends - ordered
    dest_start = jnp.sum(onehot * image_starts[:, None], axis=0)
    send_live = within[None, :] < lens_row[:, None]
    send_index = jnp.where(send_live, dest_start[:, None] + within[None, :], 0).reshape(-1)
    qkv_slots = jnp.where(
        send_live[:, :, None], jnp.take(qkv, send_index, axis=0).reshape(groups, slot_rows, -1), 0
    )
    cot_slots = jnp.where(
        send_live[:, :, None],
        jnp.take(embed_grad, send_index, axis=0).reshape(groups, slot_rows, -1),
        0,
    )
    recv_qkv, recv_cot = (
        lax.all_to_all(qkv_slots, "group", split_axis=0, concat_axis=0, tiled=True),
        lax.all_to_all(cot_slots, "group", split_axis=0, concat_axis=0, tiled=True),
    )
    recv_len = lax.dynamic_index_in_dim(lens_all, own_index, 1, keepdims=False)
    recv_live = within[None, :] < recv_len[:, None]
    recv_ends = jnp.cumsum(recv_len)
    recv_starts = recv_ends - recv_len
    cut = image_cut[0, 0]
    qkv_flat = recv_qkv.reshape(groups * slot_rows, 3 * head_feats)
    cot_flat = recv_cot.reshape(groups * slot_rows, width)
    live = recv_live.reshape(-1)
    slot_pos = (recv_starts[:, None] + within[None, :]).reshape(-1)
    second = slot_pos >= cut
    allowed = (second[:, None] == second[None, :]) & live[:, None] & live[None, :]
    embed_flat, grad_flat, att_rows = attention_pass(qkv_flat, cot_flat, out_weight, allowed, live)
    embed_slots = embed_flat.reshape(groups, slot_rows, width)
    grad_slots = grad_flat.reshape(groups, slot_rows, 3 * head_feats)
    weight_share = lax.psum_scatter(
        lax.dot_general(
            cot_flat, att_rows, (((0,), (0,)), ((), ())), preferred_element_type=jnp.float32
        ),
        "group",
        scatter_dimension=0,
        tiled=True,
    )
    weight_grad = lax.psum(weight_share, "dp")
    embed_back, grad_back = (
        lax.all_to_all(embed_slots, "group", split_axis=0, concat_axis=0, tiled=True),
        lax.all_to_all(grad_slots, "group", split_axis=0, concat_axis=0, tiled=True),
    )
    positions = jnp.arange(src_rows, dtype=jnp.int32)
    image_of = jnp.sum((image_ends[None, :] <= positions[:, None]).astype(jnp.int32), axis=1)
    row_live = (positions < image_ends[-1])[:, None]
    selector_rows = (image_of[:, None] == dest_range[None, :]).astype(jnp.int32)
    dest_of = jnp.sum(selector_rows * order_row[None, :], axis=1)
    start_of = jnp.sum(selector_rows * image_starts[None, :], axis=1)
    back_index = jnp.where(row_live[:, 0], dest_of * slot_rows + positions - start_of, 0)
    embeds = jnp.where(
        row_live, jnp.take(embed_back.reshape(groups * slot_rows, width), back_index, axis=0), 0
    )
    qkv_grad = jnp.where(
        row_live,
        jnp.take(grad_back.reshape(groups * slot_rows, 3 * head_feats), back_index, axis=0),
        0,
    )
    return (embeds, qkv_grad, weight_grad)


def solution(mesh):
    return jax.shard_map(
        local,
        mesh=mesh,
        in_specs=(
            P(("dp", "group"), None),
            P(("dp", "group"), None),
            P(),
            P("dp", None, None),
            P("dp", "group", None),
            P("dp", "group"),
        ),
        out_specs=(P(("dp", "group"), None), P(("dp", "group"), None), P("group", None)),
        check_vma=False,
    )
```

profile of v0, /device:TPU:0, one launch (start us, length us, event | category | flops | bytes accessed | tf_op | source)
XLA Modules:
  0.0 132.5 jit_solution(15237069771902360016)
XLA Ops:
  7.2 0.8 dynamic-slice_bitcast_fusion
  8.0 0.1 iota_compare_fusion.3
  8.1 0.8 select_reduce_fusion.3
  8.9 0.2 reduce-window.13
  9.1 0.7 select_reduce_fusion.2
  9.9 0.1 add_select_fusion
  10.0 0.1 select_n.57
  10.1 1.8 %gather_fusion.2 = bf16[64,1280]{1,0:T(8,128)(2,1)S(1)} fusion(bf16[64,1280]{1,0:T(8,128)(2,1)} %param.11, s32[1024]{0:T(1024)S(1)} %pad_clamp_fusion.1), kind=kCustom, calls=%fused_computation.3.clone | custom fusion | bytes 327936 | tf_op jit(solution)/shard_map/jit(_take)/gather | solution.py:91
  11.9 0.8 bitcast_select_fusion.1
  12.6 5.2 %all-to-all-start.2 = ((bf16[8,8,1280]{2,1,0:T(8,128)(2,1)}), bf16[8,8,1280]{2,1,0:T(8,128)(2,1)S(1)}, u32[]{:S(2)}, u32[]{:S(2)}) async-start(bf16[8,8,1280]{2,1,0:T(8,128)(2,1)} %bitcast_select_fusion.1), calls=%async_computation.2 | async-start | bytes 327680 | tf_op jit(solution)/shard_map/all_to_all | solution.py:96
  17.8 0.2 dynamic-slice_reduce_fusion
  18.7 0.1 iota_compare_fusion.2
  18.7 0.2 reduce-window.14
  18.9 0.1 add_compare_fusion
  19.0 0.1 ge.29
  19.1 0.1 lt.81
  19.2 0.8 gather_fusion
  19.9 0.8 bitcast_select_fusion
  20.7 0.1 and_and_fusion
  20.8 2.8 %all-to-all-done.2 = bf16[8,8,1280]{2,1,0:T(8,128)(2,1)S(1)} async-done(((bf16[8,8,1280]{2,1,0:T(8,128)(2,1)}), bf16[8,8,1280]{2,1,0:T(8,128)(2,1)S(1)}, u32[]{:S(2)}, u32[]{:S(2)}) %all-to-all-start.2) | async-done | bytes 163872 | tf_op jit(solution)/shard_map/all_to_all | solution.py:96
  23.7 3.4 %all-to-all-start = ((bf16[8,8,1920]{2,1,0:T(8,128)(2,1)}), bf16[8,8,1920]{2,1,0:T(8,128)(2,1)S(1)}, u32[]{:S(2)}, u32[]{:S(2)}) async-start(bf16[8,8,1920]{2,1,0:T(8,128)(2,1)} %bitcast_select_fusion), calls=%async_computation | async-start | bytes 491520 | tf_op jit(solution)/shard_map/all_to_all | solution.py:95
  27.1 0.0 reduce-scatter.2.cloned.1.call-start
  27.1 0.4 convolution_convert_fusion.5
  27.5 0.2 reshape.299
  27.7 6.0 %all-to-all-done = bf16[8,8,1920]{2,1,0:T(8,128)(2,1)S(1)} async-done(((bf16[8,8,1920]{2,1,0:T(8,128)(2,1)}), bf16[8,8,1920]{2,1,0:T(8,128)(2,1)S(1)}, u32[]{:S(2)}, u32[]{:S(2)}) %all-to-all-start) | async-done | bytes 245792 | tf_op jit(solution)/shard_map/all_to_all | solution.py:95
  33.8 0.2 reshape.292
  33.9 0.2 reshape.293
  34.1 0.2 reshape.289
  34.3 0.2 fusion.5
  34.5 0.4 fusion.27
  34.8 0.4 multiply_reduce_fusion
  35.2 0.1 copy.32
  35.3 0.1 reshape.294
  35.5 2.3 %fusion.12 = f32[1280,640]{1,0:T(8,128)} fusion(bf16[64,640]{1,0:T(8,128)(2,1)S(1)} %reshape.294, bf16[8,8,1280]{2,1,0:T(8,128)(2,1)S(1)} %all-to-all-done.2), kind=kOutput, calls=%fused_computation.29 | convolution fusion | flops 104857600 | bytes 3522560 | tf_op jit(solution)/shard_map/dot_general | solution.py:113
  37.8 0.0 reduce-scatter.2.cloned.1.call-update
  37.8 0.6 slice.13
  38.4 0.6 iota_compare_fusion.5
  39.0 0.1 convert_reduce_fusion
  39.1 0.1 select_reduce_fusion.1
  39.2 0.7 compare_and_fusion
  39.9 0.2 fusion.7
  40.1 0.2 fusion.9
  40.3 0.1 copy.39
  40.4 0.1 concatenate.10
  40.6 0.2 fusion.10
  40.7 0.1 copy.41
  40.8 0.1 concatenate.11
  41.0 0.2 fusion.11
  41.2 0.1 copy.43
  41.3 0.1 concatenate.12
  41.4 1.3 fusion.1
  42.7 3.4 %all-to-all-start.1 = ((bf16[8,8,1280]{2,1,0:T(8,128)(2,1)}), bf16[8,8,1280]{2,1,0:T(8,128)(2,1)S(1)}, u32[]{:S(2)}, u32[]{:S(2)}) async-start(bf16[8,8,1280]{2,1,0:T(8,128)(2,1)} %fusion.1), calls=%async_computation.1 | async-start | bytes 327680 | tf_op jit(solution)/shard_map/all_to_all | solution.py:122
  46.1 0.7 pad_maximum_fusion
  46.8 5.1 %all-to-all-done.1 = bf16[8,8,1280]{2,1,0:T(8,128)(2,1)S(1)} async-done(((bf16[8,8,1280]{2,1,0:T(8,128)(2,1)}), bf16[8,8,1280]{2,1,0:T(8,128)(2,1)S(1)}, u32[]{:S(2)}, u32[]{:S(2)}) %all-to-all-start.1) | async-done | bytes 163872 | tf_op jit(solution)/shard_map/all_to_all | solution.py:122
  51.9 3.4 %all-to-all-start.3 = ((bf16[8,8,1920]{2,1,0:T(8,128)(2,1)}), bf16[8,8,1920]{2,1,0:T(8,128)(2,1)S(1)}, u32[]{:S(2)}, u32[]{:S(2)}) async-start(bf16[8,8,1920]{2,1,0:T(8,128)(2,1)} %pad_maximum_fusion), calls=%async_computation.3 | async-start | bytes 491520 | tf_op jit(solution)/shard_map/all_to_all | solution.py:123
  55.3 0.0 all-reduce.2.cloned.1.call-start
  55.4 0.7 gather_fusion.1
  56.1 0.8 select_select_fusion.1
  56.8 5.3 %all-to-all-done.3 = bf16[8,8,1920]{2,1,0:T(8,128)(2,1)S(1)} async-done(((bf16[8,8,1920]{2,1,0:T(8,128)(2,1)}), bf16[8,8,1920]{2,1,0:T(8,128)(2,1)S(1)}, u32[]{:S(2)}, u32[]{:S(2)}) %all-to-all-start.3) | async-done | bytes 245792 | tf_op jit(solution)/shard_map/all_to_all | solution.py:123
  62.1 0.7 gather_fusion.3
  62.9 21.6 %reduce-scatter.2.cloned.1.call-done = f32[160,640]{1,0:T(8,128)} async-done(((f32[1280,640]{1,0:T(8,128)}), f32[160,640]{1,0:T(8,128)}) %reduce-scatter.2.cloned.1.call-update) | async-done | bytes 409616 | tf_op jit(solution)/shard_map/reduce_scatter | solution.py:112
  84.5 0.8 select_select_fusion
  85.3 38.6 %all-reduce.2.cloned.1.call-done = f32[160,640]{1,0:T(8,128)} async-done(((f32[160,640]{1,0:T(8,128)}), f32[160,640]{1,0:T(8,128)}) %all-reduce.2.cloned.1.call-update) | async-done | bytes 409616 | tf_op jit(solution)/shard_map/psum | solution.py:120
  123.9 1.8 %copy.68 = f32[160,640]{1,0:T(8,128)} copy(f32[160,640]{1,0:T(8,128)} %all-reduce.2.cloned.1.call-done) | data formatting | bytes 819200
  (16 shorter events, 0.1 us)
Async XLA Ops:
  7.2 20.0 %copy-start = (bf16[1280,640]{1,0:T(8,128)(2,1)S(1)}, bf16[1280,640]{1,0:T(8,128)(2,1)}, u32[]{:S(2)}) copy-start(bf16[1280,640]{1,0:T(8,128)(2,1)} %param.12) | copy-start | bytes 4915204
  7.2 10.6 %copy-start.2 = (s32[1,8,8]{2,1,0:T(8,128)S(1)}, s32[1,8,8]{2,1,0:T(8,128)}, u32[]{:S(2)}) copy-start(s32[1,8,8]{2,1,0:T(8,128)} %param.13) | copy-start | bytes 772
  7.2 12.0 %copy-start.1 = (bf16[64,1920]{1,0:T(8,128)(2,1)S(1)}, bf16[64,1920]{1,0:T(8,128)(2,1)}, u32[]{:S(2)}) copy-start(bf16[64,1920]{1,0:T(8,128)(2,1)} %param.10) | copy-start | bytes 737284
  12.6 11.0 %all-to-all-start.2 = ((bf16[8,8,1280]{2,1,0:T(8,128)(2,1)}), bf16[8,8,1280]{2,1,0:T(8,128)(2,1)S(1)}, u32[]{:S(2)}, u32[]{:S(2)}) async-start(bf16[8,8,1280]{2,1,0:T(8,128)(2,1)} %bitcast_select_fusion.1), calls=%async_computation.2 | async-start | bytes 327680 | tf_op jit(solution)/shard_map/all_to_all | solution.py:96
  23.7 10.1 %all-to-all-start = ((bf16[8,8,1920]{2,1,0:T(8,128)(2,1)}), bf16[8,8,1920]{2,1,0:T(8,128)(2,1)S(1)}, u32[]{:S(2)}, u32[]{:S(2)}) async-start(bf16[8,8,1920]{2,1,0:T(8,128)(2,1)} %bitcast_select_fusion), calls=%async_computation | async-start | bytes 491520 | tf_op jit(solution)/shard_map/all_to_all | solution.py:95
  27.1 57.4 %reduce-scatter.2.cloned.1.call-start = ((), (), s32[]{:S(2)}) async-start(), calls=%async_computation.5 | async-start | bytes 3686400 | tf_op jit(solution)/shard_map/reduce_scatter | solution.py:112
  37.8 1.4 %copy-start.3 = (s32[1,1,8]{2,1,0:T(1,128)S(1)}, s32[1,1,8]{2,1,0:T(1,128)}, u32[]{:S(2)}) copy-start(s32[1,1,8]{2,1,0:T(1,128)} %param.14) | copy-start | bytes 100
  42.7 9.2 %all-to-all-start.1 = ((bf16[8,8,1280]{2,1,0:T(8,128)(2,1)}), bf16[8,8,1280]{2,1,0:T(8,128)(2,1)S(1)}, u32[]{:S(2)}, u32[]{:S(2)}) async-start(bf16[8,8,1280]{2,1,0:T(8,128)(2,1)} %fusion.1), calls=%async_computation.1 | async-start | bytes 327680 | tf_op jit(solution)/shard_map/all_to_all | solution.py:122
  51.9 10.2 %all-to-all-start.3 = ((bf16[8,8,1920]{2,1,0:T(8,128)(2,1)}), bf16[8,8,1920]{2,1,0:T(8,128)(2,1)S(1)}, u32[]{:S(2)}, u32[]{:S(2)}) async-start(bf16[8,8,1920]{2,1,0:T(8,128)(2,1)} %pad_maximum_fusion), calls=%async_computation.3 | async-start | bytes 491520 | tf_op jit(solution)/shard_map/all_to_all | solution.py:123
  55.3 68.6 %all-reduce.2.cloned.1.call-start = ((), (), s32[]{:S(2)}) async-start(), calls=%async_computation.6 | async-start | bytes 819200 | tf_op jit(solution)/shard_map/psum | solution.py:120
Sparse Core Ops, SparseCore 0:
  37.9 46.4 reduce-scatter.1
  86.8 37.0 all-reduce.1
where the time goes:
time: 133 us
  waiting for transfers between devices  79.4 us (60%)
  starting transfers between devices  15.5 us (12%)
  between operations  15 us (11%)
  local copies, waits for them, and re-layouts  9.25 us (7%)
  other arithmetic  8.04 us (6%)
  matrix products  5.36 us (4%)
    psum x1, waiting for transfers between devices, local(): weight_grad = lax.psum(weight_share, 'dp')  38.6 us
    reduce_scatter x1, waiting for transfers between devices, local(): lax.psum_scatter(lax.dot_general(cot_flat, att_rows, (((0,), (0,)), ((),...  21.6 us
    all_to_all x1, waiting for transfers between devices, local(): lax.all_to_all(qkv_slots, 'group', split_axis=0, concat_axis=0, tiled=True)  6.03 us
    all_to_all x1, waiting for transfers between devices, local(): lax.all_to_all(grad_slots, 'group', split_axis=0, concat_axis=0, tiled=True)  5.26 us
    all_to_all x1, starting transfers between devices, local(): lax.all_to_all(cot_slots, 'group', split_axis=0, concat_axis=0, tiled=True)  5.2 us
    all_to_all x1, waiting for transfers between devices, local(): lax.all_to_all(embed_slots, 'group', split_axis=0, concat_axis=0, tiled=T...  5.07 us
    all_to_all x1, starting transfers between devices, local(): lax.all_to_all(qkv_slots, 'group', split_axis=0, concat_axis=0, tiled=True)  3.41 us
    all_to_all x1, starting transfers between devices, local(): lax.all_to_all(grad_slots, 'group', split_axis=0, concat_axis=0, tiled=True)  3.41 us
  transfers between devices with their start and end apart: 6, of which 6 were waited for; matrix products, arithmetic and copies ran while one was open for 9% of the time, Pallas kernels for 0%

commit v1 on v0

v1 whole, which is shorter than its diff:
```python
import functools
import math

import jax
import jax.numpy as jnp
from jax import lax
from jax.experimental import pallas as pl
from jax.experimental.pallas import tpu as pltpu
from jax.sharding import PartitionSpec as P

HD = 80
HEADS = 8
SLOT = 8
CHUNKS = 5
MASKED = -1e30
F32 = jnp.float32
BF16 = jnp.bfloat16
MESH = pl.DeviceIdType.MESH


def dot(a, b, dims=((1,), (0,))):
    return lax.dot_general(a, b, (dims, ((), ())), preferred_element_type=F32)


TN = ((0,), (0,))
NT = ((1,), (1,))


def iota(shape, dim):
    return lax.broadcasted_iota(jnp.int32, shape, dim)


def flat(x):
    g, s, c = x.shape
    return x.astype(F32).reshape(g * s, c).astype(BF16)


def partner(me, k):
    out, bit = me, 1
    while bit <= k:
        if k & bit:
            has = lax.rem(lax.div(me, bit), 2)
            out = out + bit * (1 - 2 * has)
        bit *= 2
    return out


def kernel(
    groups, reps,
    len_ref, order_ref, cut_ref, qkv_hbm, cot_hbm, w_hbm,
    emb_hbm, grad_hbm, wg_hbm,
    qkv, cot, w, sel, pack_t,
    sendq, recvq, sendg, recvg, cots, cotr, qbig, gbig, attall,
    grads, backs, backr, packed_cot, wgs, own, zsend, zbuf, emb, grad,
    in_sem, out_sem, loc_sem,
    sq, rq, sg, rg, sc, rc, sa, ra, sb, rb, sz, rz,
):
    me = lax.axis_index("group")
    rep = lax.axis_index("dp")
    rows, feats3 = qkv.shape
    hf = feats3 // 3
    width = cot.shape[1]
    slots = groups * SLOT
    pack = slots // 2
    share = width // groups
    tiles = width // 128

    loads = [
        pltpu.make_async_copy(qkv_hbm, qkv, in_sem.at[0]),
        pltpu.make_async_copy(cot_hbm, cot, in_sem.at[1]),
        pltpu.make_async_copy(w_hbm, w, in_sem.at[2]),
    ]
    for load in loads:
        load.start()

    barrier = pltpu.get_barrier_semaphore()
    order_k = list(range(groups - 1, 0, -1))
    for k in order_k:
        pl.semaphore_signal(
            barrier, inc=1, device_id={"group": partner(me, k)}, device_id_type=MESH
        )

    @pl.when(rep > 0)
    def _():
        pl.semaphore_signal(barrier, inc=1, device_id={"dp": rep - 1}, device_id_type=MESH)

    @pl.when(rep < reps - 1)
    def _():
        pl.semaphore_signal(barrier, inc=1, device_id={"dp": rep + 1}, device_id_type=MESH)

    sub = iota((groups, groups), 0)
    lane = iota((groups, groups), 1)
    eye = sub == lane
    lens = len_ref[...].astype(F32)
    lens_row = jnp.sum(jnp.where(sub == me, lens, 0.0), axis=0, keepdims=True)
    order_row = order_ref[...].astype(F32)
    order_col = jnp.sum(
        jnp.where(eye, jnp.broadcast_to(order_row, eye.shape), 0.0), axis=1, keepdims=True
    )
    onehot = jnp.where(order_col == lane.astype(F32), 1.0, 0.0)
    ordered_col = jnp.sum(onehot * lens_row, axis=1, keepdims=True)
    ordered_row = jnp.sum(jnp.where(eye, ordered_col, 0.0), axis=0, keepdims=True)
    starts_col = jnp.sum(
        jnp.where(lane < sub, jnp.broadcast_to(ordered_row, eye.shape), 0.0),
        axis=1, keepdims=True,
    )
    dest_row = jnp.sum(onehot * starts_col, axis=0, keepdims=True)
    block_of = iota((slots, groups), 0) // SLOT == iota((slots, groups), 1)
    within = lax.rem(iota((slots, 1), 0), SLOT).astype(F32)
    send_start = jnp.sum(jnp.where(block_of, dest_row, 0.0), axis=1, keepdims=True)
    send_len = jnp.sum(jnp.where(block_of, lens_row, 0.0), axis=1, keepdims=True)
    send_pos = jnp.where(within < send_len, send_start + within, -1.0)
    sel[...] = jnp.where(send_pos == iota((slots, rows), 1).astype(F32), 1.0, 0.0).astype(BF16)

    before = jnp.where(lane < sub, 1.0, 0.0).astype(BF16)
    lens_b = lens.astype(BF16)
    starts = dot(before, lens_b)
    expand = jnp.where(block_of, 1.0, 0.0).astype(BF16)
    pos_all = dot(expand, starts.astype(BF16)) + within
    pos_all = jnp.where(within < dot(expand, lens_b), pos_all, -1.0)
    lane_sg = iota((slots, groups), 1)
    pos_me = jnp.sum(jnp.where(lane_sg == me, pos_all, 0.0), axis=1, keepdims=True)
    packs = iota((slots, pack), 1).astype(F32)
    pack_t[...] = jnp.where(pos_me == packs, 1.0, 0.0).astype(BF16)

    def remote(src, dst, ssem, rsem, k):
        return pltpu.make_async_remote_copy(
            src_ref=src, dst_ref=dst, send_sem=ssem, recv_sem=rsem,
            device_id={"group": partner(me, k)}, device_id_type=MESH,
        )

    loads[0].wait()
    sendq[...] = dot(sel[...], qkv[...]).reshape(groups, SLOT, feats3).astype(BF16)

    pl.semaphore_wait(
        barrier,
        groups - 1 + (rep > 0).astype(jnp.int32) + (rep < reps - 1).astype(jnp.int32),
    )

    pending = []
    for k in order_k:
        copy = remote(sendq.at[partner(me, k)], recvq.at[me], sq.at[k], rq.at[k], k)
        copy.start()
        pending.append(copy)
    local_q = pltpu.make_async_copy(sendq.at[me], recvq.at[me], loc_sem.at[0])
    local_q.start()

    loads[1].wait()
    loads[2].wait()
    att_grad = dot(cot[...], w[...]).astype(BF16)
    sendg[...] = dot(sel[...], att_grad).reshape(groups, SLOT, hf).astype(BF16)
    pending_g = []
    for k in order_k:
        copy = remote(sendg.at[partner(me, k)], recvg.at[me], sg.at[k], rg.at[k], k)
        copy.start()
        pending_g.append(copy)
    local_g = pltpu.make_async_copy(sendg.at[me], recvg.at[me], loc_sem.at[1])
    local_g.start()

    cots[...] = dot(sel[...], cot[...]).reshape(groups, SLOT, width).astype(BF16)

    def window(owner):
        first = jnp.minimum(lax.div(owner * share, 128), tiles - 2)
        return first * 128

    pending_c = []
    for k in order_k:
        begin = pl.multiple_of(window(partner(me, k)), 128)
        copy = remote(cots.at[:, :, pl.ds(begin, 256)], cotr.at[me], sc.at[k], rc.at[k], k)
        copy.start()
        pending_c.append(copy)
    mine = pl.multiple_of(window(me), 128)
    local_c = pltpu.make_async_copy(
        cots.at[:, :, pl.ds(mine, 256)], cotr.at[me], loc_sem.at[2]
    )
    local_c.start()

    local_q.wait()
    for copy in pending:
        copy.wait_recv()
    xq = dot(pack_t[...], flat(recvq[...]), TN).astype(BF16)
    query, keys, values = xq[:, :hf], xq[:, hf : 2 * hf], xq[:, 2 * hf :]
    feature = iota((1, hf), 1)
    heads = [
        (feature >= h * HD) & (feature < (h + 1) * HD) for h in range(HEADS)
    ]
    marks = [jnp.where(m, 1.0, 0.0).astype(BF16) for m in heads]
    for h in range(HEADS):
        qbig[h * pack : (h + 1) * pack, :] = query * marks[h]
    scale = 1.0 / math.sqrt(HD)
    cut = cut_ref[0, 0]
    wide = HEADS * pack
    row_second = iota((pack, wide), 0) >= cut
    col_second = lax.rem(iota((pack, wide), 1), pack) >= cut
    same = row_second == col_second
    scores = dot(keys, qbig[...], NT) * scale
    scores = jnp.where(same, scores, MASKED)
    top = jnp.max(scores, axis=0, keepdims=True)
    expo = jnp.exp(scores - top)
    probs = expo / jnp.sum(expo, axis=0, keepdims=True)
    probs_b = probs.astype(BF16)

    def per_head(big):
        out = jnp.where(heads[0], big[:pack], 0.0)
        for h in range(1, HEADS):
            out = jnp.where(heads[h], big[h * pack : (h + 1) * pack], out)
        return out.astype(BF16)

    att = per_head(dot(probs_b, values, TN))
    attall[pl.ds(me, 1)] = att.reshape(1, pack, hf)
    pending_a = []
    for k in order_k:
        copy = remote(attall.at[me], attall.at[me], sa.at[k], ra.at[k], k)
        copy.start()
        pending_a.append(copy)
    grads[:, :hf] = att

    local_g.wait()
    for copy in pending_g:
        copy.wait_recv()
    xg = dot(pack_t[...], flat(recvg[...]), TN).astype(BF16)
    for h in range(HEADS):
        gbig[h * pack : (h + 1) * pack, :] = xg * marks[h]
    prob_grad = dot(values, gbig[...], NT)
    delta = jnp.sum(probs * prob_grad, axis=0, keepdims=True)
    score_grad = (probs * (prob_grad - delta) * scale).astype(BF16)
    grads[:, hf : 2 * hf] = per_head(dot(score_grad, keys, TN))
    grads[:, 2 * hf : 3 * hf] = dot(score_grad, qbig[...]).astype(BF16)
    grads[:, 3 * hf :] = dot(probs_b, gbig[...]).astype(BF16)

    backs[...] = dot(pack_t[...], grads[...]).reshape(groups, SLOT, 4 * hf).astype(BF16)
    pending_b = []
    for k in order_k:
        copy = remote(backs.at[partner(me, k)], backr.at[me], sb.at[k], rb.at[k], k)
        copy.start()
        pending_b.append(copy)
    local_b = pltpu.make_async_copy(backs.at[me], backr.at[me], loc_sem.at[3])
    local_b.start()

    local_c.wait()
    for copy in pending_c:
        copy.wait_recv()
    for d in range(groups):
        place = jnp.where(pos_all[:, d : d + 1] == packs, 1.0, 0.0).astype(BF16)
        packed_cot[d * pack : (d + 1) * pack, :] = dot(
            place, flat(cotr[:, d]), TN
        ).astype(BF16)
    for copy in pending_a:
        copy.wait_recv()
    wgs[...] = dot(packed_cot[...], attall[...].reshape(groups * pack, hf), TN)
    offset = pl.multiple_of(me * share - window(me), 8)
    own[...] = wgs[pl.ds(offset, share), :].reshape(own.shape)

    @pl.when(rep == 0)
    def _():
        zbuf[0] = jnp.zeros(zbuf.shape[1:], BF16)

    @pl.when(rep == reps - 1)
    def _():
        zbuf[1] = jnp.zeros(zbuf.shape[1:], BF16)

    def hop(way, c):
        return pltpu.make_async_remote_copy(
            src_ref=zsend.at[way, c], dst_ref=zbuf.at[way, c],
            send_sem=sz.at[way, c], recv_sem=rz.at[way, c],
            device_id={"dp": rep + 1 - 2 * way}, device_id_type=MESH,
        )

    def step(way, c):
        spot = rep + way * (reps - 1 - 2 * rep)

        @pl.when(spot > 0)
        def _():
            hop(way, c).wait_recv()

        @pl.when(spot < reps - 1)
        def _():
            zsend[way, c] = (own[c] + zbuf[way, c].astype(F32)).astype(BF16)
            hop(way, c).start()

    near = (rep >= reps // 2).astype(jnp.int32)
    lag = 2
    for t in range(CHUNKS + lag):
        if t < CHUNKS:
            step(near, t)
        if t >= lag:
            step(1 - near, t - lag)

    local_b.wait()
    for copy in pending_b:
        copy.wait_recv()
    back = dot(sel[...], flat(backr[...]), TN).astype(BF16)
    grad[...] = back[:, hf:]
    store_g = pltpu.make_async_copy(grad, grad_hbm, out_sem.at[1])
    store_g.start()
    emb[...] = dot(back[:, :hf], w[...], NT).astype(BF16)
    store_e = pltpu.make_async_copy(emb, emb_hbm, out_sem.at[0])
    store_e.start()

    own[...] = own[...] + zbuf[0].astype(F32) + zbuf[1].astype(F32)
    store_w = pltpu.make_async_copy(own, wg_hbm, out_sem.at[2])
    store_w.start()

    for copies in (pending, pending_g, pending_c, pending_a, pending_b):
        for copy in copies:
            copy.wait_send()
    for way in range(2):
        spot = rep + way * (reps - 1 - 2 * rep)

        @pl.when(spot < reps - 1)
        def _():
            for c in range(CHUNKS):
                hop(way, c).wait_send()

    store_g.wait()
    store_e.wait()
    store_w.wait()


def local(groups, reps, qkv, embed_grad, out_weight, image_len, image_order, image_cut):
    rows, feats3 = qkv.shape
    width, hf = out_weight.shape
    slots = groups * SLOT
    pack = slots // 2
    share = width // groups
    part = share // CHUNKS
    any_space = pl.BlockSpec(memory_space=pl.ANY)
    vmem = pl.BlockSpec(memory_space=pltpu.VMEM)
    smem = pl.BlockSpec(memory_space=pltpu.SMEM)
    dma = pltpu.SemaphoreType.DMA
    emb, grad, wg = pl.pallas_call(
        functools.partial(kernel, groups, reps),
        out_shape=(
            jax.ShapeDtypeStruct((rows, width), BF16),
            jax.ShapeDtypeStruct((rows, feats3), BF16),
            jax.ShapeDtypeStruct((CHUNKS, part, hf), F32),
        ),
        in_specs=[vmem, vmem, smem, any_space, any_space, any_space],
        out_specs=(any_space, any_space, any_space),
        scratch_shapes=[
            pltpu.VMEM((rows, feats3), BF16),
            pltpu.VMEM((rows, width), BF16),
            pltpu.VMEM((width, hf), BF16),
            pltpu.VMEM((slots, rows), BF16),
            pltpu.VMEM((slots, pack), BF16),
            pltpu.VMEM((groups, SLOT, feats3), BF16),
            pltpu.VMEM((groups, SLOT, feats3), BF16),
            pltpu.VMEM((groups, SLOT, hf), BF16),
            pltpu.VMEM((groups, SLOT, hf), BF16),
            pltpu.VMEM((groups, SLOT, width), BF16),
            pltpu.VMEM((groups, groups, SLOT, 256), BF16),
            pltpu.VMEM((HEADS * pack, hf), BF16),
            pltpu.VMEM((HEADS * pack, hf), BF16),
            pltpu.VMEM((groups, pack, hf), BF16),
            pltpu.VMEM((pack, 4 * hf), BF16),
            pltpu.VMEM((groups, SLOT, 4 * hf), BF16),
            pltpu.VMEM((groups, SLOT, 4 * hf), BF16),
            pltpu.VMEM((groups * pack, 256), BF16),
            pltpu.VMEM((256, hf), F32),
            pltpu.VMEM((CHUNKS, part, hf), F32),
            pltpu.VMEM((2, CHUNKS, part, hf), BF16),
            pltpu.VMEM((2, CHUNKS, part, hf), BF16),
            pltpu.VMEM((rows, width), BF16),
            pltpu.VMEM((rows, feats3), BF16),
            dma((3,)), dma((3,)), dma((4,)),
        ]
        + [dma((groups,)) for _ in range(10)]
        + [dma((2, CHUNKS)), dma((2, CHUNKS))],
        compiler_params=pltpu.CompilerParams(
            collective_id=0, has_side_effects=True, vmem_limit_bytes=60 * 1024 * 1024
        ),
    )(
        image_len.reshape(groups, groups), image_order.reshape(1, groups), image_cut,
        qkv, embed_grad, out_weight,
    )
    return emb, grad, wg.reshape(share, hf)


def solution(mesh):
    return jax.shard_map(
        functools.partial(local, mesh.shape["group"], mesh.shape["dp"]),
        mesh=mesh,
        in_specs=(
            P(("dp", "group"), None),
            P(("dp", "group"), None),
            P(),
            P("dp", None, None),
            P("dp", "group", None),
            P("dp", "group"),
        ),
        out_specs=(P(("dp", "group"), None), P(("dp", "group"), None), P("group", None)),
        check_vma=False,
    )
```

time: 133 us -> 51.2 us (0.38)
  waiting for transfers between devices: 79.4 us -> 0 us
  Pallas kernels: 0 us -> 44.6 us
  starting transfers between devices: 15.5 us -> 0 us
  between operations: 15 us -> 1.29 us
  other arithmetic: 8.04 us -> 0 us
  matrix products: 5.36 us -> 0 us
  local copies, waits for them, and re-layouts: 9.25 us -> 5.03 us
    pallas_call x0 -> x1, Pallas kernels: none -> 44.6 us  [local(): pl.pallas_call(functools.partial(kernel, groups, reps), out_shape=(jax.Sh...]
    psum x1 -> x0, waiting for transfers between devices: 38.6 us -> none  [local(): weight_grad = lax.psum(weight_share, 'dp')]
    reduce_scatter x1 -> x0, waiting for transfers between devices: 21.6 us -> none  [local(): lax.psum_scatter(lax.dot_general(cot_flat, att_rows, (((0,), (0,)), ((),...]
    all_to_all x4 -> x0, waiting for transfers between devices: 19.2 us -> none  [the longest x1 6.03 us: local(): lax.all_to_all(qkv_slots, 'group', split_axis=0, concat_axis=0, tiled=True)]
    all_to_all x4 -> x0, starting transfers between devices: 15.4 us -> none  [the longest x1 5.2 us: local(): lax.all_to_all(cot_slots, 'group', split_axis=0, concat_axis=0, tiled=True)]
    dot_general x9 -> x0, matrix products: 5.36 us -> none  [the longest x1 2.31 us: local(): lax.dot_general(cot_flat, att_rows, (((0,), (0,)), ((), ())), preferred_e...]
    gather x4 -> x0, local copies, waits for them, and re-layouts: 4.01 us -> none  [the longest x1 1.78 us: local(): jnp.take(embed_grad, send_index, axis=0).reshape(groups, slot_rows, -1)]
    unnamed x9 -> x3, local copies, waits for them, and re-layouts: 1.8 us -> 5.03 us
  transfers between devices with their start and end apart: 6 -> 0, of which waited for: 6 -> 0; matrix products, arithmetic and copies ran while one was open for 9% -> 0% of each run, Pallas kernels for 0% -> 0%
where the time goes in v1:
time: 51.2 us; the launch traced here: 50.9 us
  Pallas kernels  44.6 us (87%)
  local copies, waits for them, and re-layouts  5.03 us (10%)
  between operations  1.29 us (3%)
    pallas_call x1, Pallas kernels, local(): pl.pallas_call(functools.partial(kernel, groups, reps), out_shape=(jax.Sh...  44.6 us
    unnamed x3, local copies, waits for them, and re-layouts  5.03 us

profile of v1, /device:TPU:0, one launch (start us, length us, event | category | flops | bytes accessed | tf_op | source)
XLA Modules:
  0.0 50.9 jit_solution(10942695946644263674)
XLA Ops:
  1.3 44.6 %shard_map.85 = (bf16[64,1280]{1,0:T(8,128)(2,1)}, bf16[64,1920]{1,0:T(8,128)(2,1)}, f32[5,32,640]{2,1,0:T(8,128)}) custom-call(s32[8,8]{1,0:T(8,128)} %bitcast.4, s32[1,8]{1,0:T(1,128)} %bitcast.5, s32[1,1]{1,0:T(1,128)S(6)} %copy.12.cut_ref, bf16[64,1920]{1,0:T(8,128)(2,1)} %qkv_hbm.1, bf16[64,1280]{1,0:T(8,128)(2,1)} %cot_hbm.1, bf16[1280,640]{1,0:T(8,128)(2,1)} %w_hbm.1), custom_call_target="tpu_custom_call" | custom-call | tf_op jit(solution)/shard_map/pallas_call | solution.py:331
  45.9 1.6 %copy.13 = bf16[64,1280]{1,0:T(8,128)(2,1)} copy(bf16[64,1280]{1,0:T(8,128)(2,1)} %get-tuple-element.12) | data formatting | bytes 327680
  47.5 1.7 %copy.14 = bf16[64,1920]{1,0:T(8,128)(2,1)} copy(bf16[64,1920]{1,0:T(8,128)(2,1)} %get-tuple-element.13) | data formatting | bytes 491520
  49.2 1.8 %copy.15 = f32[160,640]{1,0:T(8,128)} copy(f32[160,640]{1,0:T(8,128)} %bitcast.3) | data formatting | bytes 819200

commit v2 on v1

--- a/solution.py
+++ b/solution.py
@@ -18,6 +18,20 @@
 MESH = pl.DeviceIdType.MESH
 
 
+TRACE = False
+open_scope = []
+
+
+def mark(name):
+    if TRACE:
+        if open_scope:
+            open_scope.pop().__exit__(None, None, None)
+        if name:
+            scope = jax.named_scope(name)
+            scope.__enter__()
+            open_scope.append(scope)
+
+
 def dot(a, b, dims=((1,), (0,))):
     return lax.dot_general(a, b, (dims, ((), ())), preferred_element_type=F32)
 
@@ -48,11 +62,11 @@
 def kernel(
     groups, reps,
     len_ref, order_ref, cut_ref, qkv_hbm, cot_hbm, w_hbm,
-    emb_hbm, grad_hbm, wg_hbm,
+    emb, grad, own,
     qkv, cot, w, sel, pack_t,
     sendq, recvq, sendg, recvg, cots, cotr, qbig, gbig, attall,
-    grads, backs, backr, packed_cot, wgs, own, zsend, zbuf, emb, grad,
-    in_sem, out_sem, loc_sem,
+    grads, backs, backr, packed_cot, wgs, zsend, zbuf,
+    in_sem, loc_sem,
     sq, rq, sg, rg, sc, rc, sa, ra, sb, rb, sz, rz,
 ):
     me = lax.axis_index("group")
@@ -65,6 +79,7 @@
     share = width // groups
     tiles = width // 128
 
+    mark("m00_start")
     loads = [
         pltpu.make_async_copy(qkv_hbm, qkv, in_sem.at[0]),
         pltpu.make_async_copy(cot_hbm, cot, in_sem.at[1]),
@@ -88,6 +103,7 @@
     def _():
         pl.semaphore_signal(barrier, inc=1, device_id={"dp": rep + 1}, device_id_type=MESH)
 
+    mark("m01_book")
     sub = iota((groups, groups), 0)
     lane = iota((groups, groups), 1)
     eye = sub == lane
@@ -129,14 +145,17 @@
             device_id={"group": partner(me, k)}, device_id_type=MESH,
         )
 
+    mark("m02_selq")
     loads[0].wait()
     sendq[...] = dot(sel[...], qkv[...]).reshape(groups, SLOT, feats3).astype(BF16)
 
+    mark("m03_barrier")
     pl.semaphore_wait(
         barrier,
         groups - 1 + (rep > 0).astype(jnp.int32) + (rep < reps - 1).astype(jnp.int32),
     )
 
+    mark("m04_sendq")
     pending = []
     for k in order_k:
         copy = remote(sendq.at[partner(me, k)], recvq.at[me], sq.at[k], rq.at[k], k)
@@ -145,6 +164,7 @@
     local_q = pltpu.make_async_copy(sendq.at[me], recvq.at[me], loc_sem.at[0])
     local_q.start()
 
+    mark("m05_attgrad")
     loads[1].wait()
     loads[2].wait()
     att_grad = dot(cot[...], w[...]).astype(BF16)
@@ -157,6 +177,7 @@
     local_g = pltpu.make_async_copy(sendg.at[me], recvg.at[me], loc_sem.at[1])
     local_g.start()
 
+    mark("m06_cot")
     cots[...] = dot(sel[...], cot[...]).reshape(groups, SLOT, width).astype(BF16)
 
     def window(owner):
@@ -175,9 +196,11 @@
     )
     local_c.start()
 
+    mark("m07_waitq")
     local_q.wait()
     for copy in pending:
         copy.wait_recv()
+    mark("m08_att")
     xq = dot(pack_t[...], flat(recvq[...]), TN).astype(BF16)
     query, keys, values = xq[:, :hf], xq[:, hf : 2 * hf], xq[:, 2 * hf :]
     feature = iota((1, hf), 1)
@@ -215,9 +238,11 @@
         pending_a.append(copy)
     grads[:, :hf] = att
 
+    mark("m09_waitg")
     local_g.wait()
     for copy in pending_g:
         copy.wait_recv()
+    mark("m10_bwd")
     xg = dot(pack_t[...], flat(recvg[...]), TN).astype(BF16)
     for h in range(HEADS):
         gbig[h * pack : (h + 1) * pack, :] = xg * marks[h]
@@ -237,20 +262,25 @@
     local_b = pltpu.make_async_copy(backs.at[me], backr.at[me], loc_sem.at[3])
     local_b.start()
 
+    mark("m11_waitc")
     local_c.wait()
     for copy in pending_c:
         copy.wait_recv()
+    mark("m12_pack")
     for d in range(groups):
         place = jnp.where(pos_all[:, d : d + 1] == packs, 1.0, 0.0).astype(BF16)
         packed_cot[d * pack : (d + 1) * pack, :] = dot(
             place, flat(cotr[:, d]), TN
         ).astype(BF16)
+    mark("m13_waita")
     for copy in pending_a:
         copy.wait_recv()
+    mark("m14_wg")
     wgs[...] = dot(packed_cot[...], attall[...].reshape(groups * pack, hf), TN)
     offset = pl.multiple_of(me * share - window(me), 8)
     own[...] = wgs[pl.ds(offset, share), :].reshape(own.shape)
 
+    mark("m15_zchain")
     @pl.when(rep == 0)
     def _():
         zbuf[0] = jnp.zeros(zbuf.shape[1:], BF16)
@@ -278,29 +308,42 @@
             zsend[way, c] = (own[c] + zbuf[way, c].astype(F32)).astype(BF16)
             hop(way, c).start()
 
-    near = (rep >= reps // 2).astype(jnp.int32)
-    lag = 2
-    for t in range(CHUNKS + lag):
-        if t < CHUNKS:
-            step(near, t)
-        if t >= lag:
-            step(1 - near, t - lag)
-
-    local_b.wait()
-    for copy in pending_b:
-        copy.wait_recv()
-    back = dot(sel[...], flat(backr[...]), TN).astype(BF16)
-    grad[...] = back[:, hf:]
-    store_g = pltpu.make_async_copy(grad, grad_hbm, out_sem.at[1])
-    store_g.start()
-    emb[...] = dot(back[:, :hf], w[...], NT).astype(BF16)
-    store_e = pltpu.make_async_copy(emb, emb_hbm, out_sem.at[0])
-    store_e.start()
-
+    def source_rows():
+        mark("m16_waitb")
+        local_b.wait()
+        for copy in pending_b:
+            copy.wait_recv()
+        mark("m17_back")
+        back = dot(sel[...], flat(backr[...]), TN).astype(BF16)
+        grad[...] = back[:, hf:]
+        emb[...] = dot(back[:, :hf], w[...], NT).astype(BF16)
+        mark("m175")
+
+    near = (rep >= (reps + 1) // 2).astype(jnp.int32)
+    edge = (rep == 0) | (rep == reps - 1)
+
+    @pl.when(edge)
+    def _():
+        for c in range(CHUNKS):
+            step(near, c)
+        source_rows()
+        for c in range(CHUNKS):
+            step(1 - near, c)
+
+    @pl.when(jnp.logical_not(edge))
+    def _():
+        lag = 2
+        for t in range(CHUNKS + lag):
+            if t < CHUNKS:
+                step(near, t)
+            if t >= lag:
+                step(1 - near, t - lag)
+        source_rows()
+
+    mark("m18_final")
     own[...] = own[...] + zbuf[0].astype(F32) + zbuf[1].astype(F32)
-    store_w = pltpu.make_async_copy(own, wg_hbm, out_sem.at[2])
-    store_w.start()
-
+
+    mark("m19_drain")
     for copies in (pending, pending_g, pending_c, pending_a, pending_b):
         for copy in copies:
             copy.wait_send()
@@ -312,9 +355,18 @@
             for c in range(CHUNKS):
                 hop(way, c).wait_send()
 
-    store_g.wait()
-    store_e.wait()
-    store_w.wait()
+    mark(None)
+
+
+def write_out(emb, grad, own, emb_hbm, grad_hbm, wg_hbm, sems):
+    pairs = ((emb, emb_hbm), (grad, grad_hbm), (own, wg_hbm))
+    copies = [
+        pltpu.make_async_copy(src, dst, sems.at[i]) for i, (src, dst) in enumerate(pairs)
+    ]
+    for copy in copies:
+        copy.start()
+    for copy in copies:
+        copy.wait()
 
 
 def local(groups, reps, qkv, embed_grad, out_weight, image_len, image_order, image_cut):
@@ -331,12 +383,12 @@
     emb, grad, wg = pl.pallas_call(
         functools.partial(kernel, groups, reps),
         out_shape=(
-            jax.ShapeDtypeStruct((rows, width), BF16),
-            jax.ShapeDtypeStruct((rows, feats3), BF16),
-            jax.ShapeDtypeStruct((CHUNKS, part, hf), F32),
+            pltpu.VMEM((rows, width), BF16),
+            pltpu.VMEM((rows, feats3), BF16),
+            pltpu.VMEM((CHUNKS, part, hf), F32),
         ),
         in_specs=[vmem, vmem, smem, any_space, any_space, any_space],
-        out_specs=(any_space, any_space, any_space),
+        out_specs=(vmem, vmem, vmem),
         scratch_shapes=[
             pltpu.VMEM((rows, feats3), BF16),
             pltpu.VMEM((rows, width), BF16),
@@ -357,12 +409,9 @@
             pltpu.VMEM((groups, SLOT, 4 * hf), BF16),
             pltpu.VMEM((groups * pack, 256), BF16),
             pltpu.VMEM((256, hf), F32),
-            pltpu.VMEM((CHUNKS, part, hf), F32),
             pltpu.VMEM((2, CHUNKS, part, hf), BF16),
             pltpu.VMEM((2, CHUNKS, part, hf), BF16),
-            pltpu.VMEM((rows, width), BF16),
-            pltpu.VMEM((rows, feats3), BF16),
-            dma((3,)), dma((3,)), dma((4,)),
+            dma((3,)), dma((4,)),
         ]
         + [dma((groups,)) for _ in range(10)]
         + [dma((2, CHUNKS)), dma((2, CHUNKS))],
@@ -373,6 +422,17 @@
         image_len.reshape(groups, groups), image_order.reshape(1, groups), image_cut,
         qkv, embed_grad, out_weight,
     )
+    emb, grad, wg = pl.pallas_call(
+        write_out,
+        out_shape=(
+            jax.ShapeDtypeStruct((rows, width), BF16),
+            jax.ShapeDtypeStruct((rows, feats3), BF16),
+            jax.ShapeDtypeStruct((CHUNKS, part, hf), F32),
+        ),
+        in_specs=[vmem, vmem, vmem],
+        out_specs=(any_space, any_space, any_space),
+        scratch_shapes=[dma((3,))],
+    )(*(pltpu.with_memory_space_constraint(x, pltpu.VMEM) for x in (emb, grad, wg)))
     return emb, grad, wg.reshape(share, hf)
 
 

time: 51.2 us -> 33.8 us (0.66)
  Pallas kernels: 44.6 us -> 32.3 us
  local copies, waits for them, and re-layouts: 5.03 us -> 0 us
    pallas_call x1 -> x2, Pallas kernels: 44.6 us -> 32.3 us  [the longest x1 31.4 us: local(): pl.pallas_call(functools.partial(kernel, groups, reps), out_shape=(pltpu....]
    unnamed x3 -> x0, local copies, waits for them, and re-layouts: 5.03 us -> none
where the time goes in v2:
time: 33.8 us; the launch traced here: 33.6 us
  Pallas kernels  32.3 us (96%)
  between operations  1.29 us (4%)
    pallas_call x1, Pallas kernels, local(): pl.pallas_call(functools.partial(kernel, groups, reps), out_shape=(pltpu....  31.4 us
    pallas_call x1, Pallas kernels, local(): pl.pallas_call(write_out, out_shape=(jax.ShapeDtypeStruct((rows, width),...  0.92 us

profile of v2, /device:TPU:0, one launch (start us, length us, event | category | flops | bytes accessed | tf_op | source)
XLA Modules:
  0.0 33.6 jit_solution(8241863908516104430)
XLA Ops:
  1.3 31.4 %shard_map.85 = (bf16[64,1280]{1,0:T(8,128)(2,1)S(1)}, bf16[64,1920]{1,0:T(8,128)(2,1)S(1)}, f32[5,32,640]{2,1,0:T(8,128)S(1)}) custom-call(s32[8,8]{1,0:T(8,128)} %bitcast.3, s32[1,8]{1,0:T(1,128)} %bitcast.4, s32[1,1]{1,0:T(1,128)S(6)} %copy.9.cut_ref, bf16[64,1920]{1,0:T(8,128)(2,1)} %qkv_hbm.1, bf16[64,1280]{1,0:T(8,128)(2,1)} %cot_hbm.1, ...), custom_call_target="tpu_custom_call" | custom-call | tf_op jit(solution)/shard_map/pallas_call | solution.py:383
  32.7 0.9 %shard_map.86 = (bf16[64,1280]{1,0:T(8,128)(2,1)}, bf16[64,1920]{1,0:T(8,128)(2,1)}, f32[5,32,640]{2,1,0:T(8,128)}) custom-call(bf16[64,1280]{1,0:T(8,128)(2,1)S(1)} %get-tuple-element.9.emb, bf16[64,1920]{1,0:T(8,128)(2,1)S(1)} %get-tuple-element.10.grad, f32[5,32,640]{2,1,0:T(8,128)S(1)} %get-tuple-element.11.own), custom_call_target="tpu_custom_call" | custom-call | tf_op jit(solution)/shard_map/pallas_call | solution.py:425

commit v3 on v2

--- a/solution.py
+++ b/solution.py
@@ -11,7 +11,6 @@
 HD = 80
 HEADS = 8
 SLOT = 8
-CHUNKS = 5
 MASKED = -1e30
 F32 = jnp.float32
 BF16 = jnp.bfloat16
@@ -61,9 +60,9 @@
 
 def kernel(
     groups, reps,
-    len_ref, order_ref, cut_ref, qkv_hbm, cot_hbm, w_hbm,
+    len_hbm, order_hbm, cut_hbm, qkv_hbm, cot_hbm, w_hbm,
     emb, grad, own,
-    qkv, cot, w, sel, pack_t,
+    len_ref, order_ref, cut_ref, qkv, cot, w, sel, pack_t,
     sendq, recvq, sendg, recvg, cots, cotr, qbig, gbig, attall,
     grads, backs, backr, packed_cot, wgs, zsend, zbuf,
     in_sem, loc_sem,
@@ -78,16 +77,9 @@
     pack = slots // 2
     share = width // groups
     tiles = width // 128
+    chunks = zbuf.shape[1]
 
     mark("m00_start")
-    loads = [
-        pltpu.make_async_copy(qkv_hbm, qkv, in_sem.at[0]),
-        pltpu.make_async_copy(cot_hbm, cot, in_sem.at[1]),
-        pltpu.make_async_copy(w_hbm, w, in_sem.at[2]),
-    ]
-    for load in loads:
-        load.start()
-
     barrier = pltpu.get_barrier_semaphore()
     order_k = list(range(groups - 1, 0, -1))
     for k in order_k:
@@ -103,7 +95,21 @@
     def _():
         pl.semaphore_signal(barrier, inc=1, device_id={"dp": rep + 1}, device_id_type=MESH)
 
+    loads = [
+        pltpu.make_async_copy(src, dst, in_sem.at[i])
+        for i, (src, dst) in enumerate(
+            (
+                (qkv_hbm, qkv), (cot_hbm, cot), (w_hbm, w),
+                (len_hbm, len_ref), (order_hbm, order_ref), (cut_hbm, cut_ref),
+            )
+        )
+    ]
+    for i in (3, 4, 5, 0, 1, 2):
+        loads[i].start()
+
     mark("m01_book")
+    for i in (3, 4, 5):
+        loads[i].wait()
     sub = iota((groups, groups), 0)
     lane = iota((groups, groups), 1)
     eye = sub == lane
@@ -211,7 +217,7 @@
     for h in range(HEADS):
         qbig[h * pack : (h + 1) * pack, :] = query * marks[h]
     scale = 1.0 / math.sqrt(HD)
-    cut = cut_ref[0, 0]
+    cut = cut_ref[...]
     wide = HEADS * pack
     row_second = iota((pack, wide), 0) >= cut
     col_second = lax.rem(iota((pack, wide), 1), pack) >= cut
@@ -232,7 +238,7 @@
     att = per_head(dot(probs_b, values, TN))
     attall[pl.ds(me, 1)] = att.reshape(1, pack, hf)
     pending_a = []
-    for k in order_k:
+    for k in list(range(groups - 2, 0, -2)) + [1]:
         copy = remote(attall.at[me], attall.at[me], sa.at[k], ra.at[k], k)
         copy.start()
         pending_a.append(copy)
@@ -273,7 +279,15 @@
             place, flat(cotr[:, d]), TN
         ).astype(BF16)
     mark("m13_waita")
-    for copy in pending_a:
+    relayed = []
+    for k in range(2, groups, 2):
+        remote(attall.at[me], attall.at[me], sa.at[k], ra.at[k], k).wait_recv()
+        piece = attall.at[partner(me, k)]
+        copy = remote(piece, piece, sa.at[k + 1], ra.at[k + 1], 1)
+        copy.start()
+        relayed.append(copy)
+    remote(attall.at[me], attall.at[me], sa.at[1], ra.at[1], 1).wait_recv()
+    for copy in relayed:
         copy.wait_recv()
     mark("m14_wg")
     wgs[...] = dot(packed_cot[...], attall[...].reshape(groups * pack, hf), TN)
@@ -324,17 +338,17 @@
 
     @pl.when(edge)
     def _():
-        for c in range(CHUNKS):
+        for c in range(chunks):
             step(near, c)
         source_rows()
-        for c in range(CHUNKS):
+        for c in range(chunks):
             step(1 - near, c)
 
     @pl.when(jnp.logical_not(edge))
     def _():
-        lag = 2
-        for t in range(CHUNKS + lag):
-            if t < CHUNKS:
+        lag = chunks // 2
+        for t in range(chunks + lag):
+            if t < chunks:
                 step(near, t)
             if t >= lag:
                 step(1 - near, t - lag)
@@ -344,7 +358,7 @@
     own[...] = own[...] + zbuf[0].astype(F32) + zbuf[1].astype(F32)
 
     mark("m19_drain")
-    for copies in (pending, pending_g, pending_c, pending_a, pending_b):
+    for copies in (pending, pending_g, pending_c, pending_a, relayed, pending_b):
         for copy in copies:
             copy.wait_send()
     for way in range(2):
@@ -352,7 +366,7 @@
 
         @pl.when(spot < reps - 1)
         def _():
-            for c in range(CHUNKS):
+            for c in range(chunks):
                 hop(way, c).wait_send()
 
     mark(None)
@@ -375,21 +389,24 @@
     slots = groups * SLOT
     pack = slots // 2
     share = width // groups
-    part = share // CHUNKS
+    part = 16 if share % 16 == 0 else 8
+    chunks = share // part
     any_space = pl.BlockSpec(memory_space=pl.ANY)
     vmem = pl.BlockSpec(memory_space=pltpu.VMEM)
-    smem = pl.BlockSpec(memory_space=pltpu.SMEM)
     dma = pltpu.SemaphoreType.DMA
     emb, grad, wg = pl.pallas_call(
         functools.partial(kernel, groups, reps),
         out_shape=(
             pltpu.VMEM((rows, width), BF16),
             pltpu.VMEM((rows, feats3), BF16),
-            pltpu.VMEM((CHUNKS, part, hf), F32),
+            pltpu.VMEM((chunks, part, hf), F32),
         ),
-        in_specs=[vmem, vmem, smem, any_space, any_space, any_space],
+        in_specs=[any_space] * 6,
         out_specs=(vmem, vmem, vmem),
         scratch_shapes=[
+            pltpu.VMEM((groups, groups), jnp.int32),
+            pltpu.VMEM((1, groups), jnp.int32),
+            pltpu.VMEM((1, 1), jnp.int32),
             pltpu.VMEM((rows, feats3), BF16),
             pltpu.VMEM((rows, width), BF16),
             pltpu.VMEM((width, hf), BF16),
@@ -409,12 +426,12 @@
             pltpu.VMEM((groups, SLOT, 4 * hf), BF16),
             pltpu.VMEM((groups * pack, 256), BF16),
             pltpu.VMEM((256, hf), F32),
-            pltpu.VMEM((2, CHUNKS, part, hf), BF16),
-            pltpu.VMEM((2, CHUNKS, part, hf), BF16),
-            dma((3,)), dma((4,)),
+            pltpu.VMEM((2, chunks, part, hf), BF16),
+            pltpu.VMEM((2, chunks, part, hf), BF16),
+            dma((6,)), dma((4,)),
         ]
         + [dma((groups,)) for _ in range(10)]
-        + [dma((2, CHUNKS)), dma((2, CHUNKS))],
+        + [dma((2, chunks)), dma((2, chunks))],
         compiler_params=pltpu.CompilerParams(
             collective_id=0, has_side_effects=True, vmem_limit_bytes=60 * 1024 * 1024
         ),
@@ -427,7 +444,7 @@
         out_shape=(
             jax.ShapeDtypeStruct((rows, width), BF16),
             jax.ShapeDtypeStruct((rows, feats3), BF16),
-            jax.ShapeDtypeStruct((CHUNKS, part, hf), F32),
+            jax.ShapeDtypeStruct((chunks, part, hf), F32),
         ),
         in_specs=[vmem, vmem, vmem],
         out_specs=(any_space, any_space, any_space),

time: 33.8 us -> 32.6 us (0.964)
  Pallas kernels: 32.3 us -> 31.1 us
    pallas_call x1, Pallas kernels: 31.4 us -> 30.2 us  [local(): pl.pallas_call(functools.partial(kernel, groups, reps), out_shape=(pltpu....]
where the time goes in v3:
time: 32.6 us; the launch traced here: 32.4 us
  Pallas kernels  31.1 us (95%)
  between operations  1.29 us (4%)
    pallas_call x1, Pallas kernels, local(): pl.pallas_call(functools.partial(kernel, groups, reps), out_shape=(pltpu....  30.2 us
    pallas_call x1, Pallas kernels, local(): pl.pallas_call(write_out, out_shape=(jax.ShapeDtypeStruct((rows, width),...  0.92 us

profile of v3, /device:TPU:0, one launch (start us, length us, event | category | flops | bytes accessed | tf_op | source)
XLA Modules:
  0.0 32.4 jit_solution(5485900376342336363)
XLA Ops:
  1.3 30.2 %shard_map.85 = (bf16[64,1280]{1,0:T(8,128)(2,1)S(1)}, bf16[64,1920]{1,0:T(8,128)(2,1)S(1)}, f32[10,16,640]{2,1,0:T(8,128)S(1)}) custom-call(s32[8,8]{1,0:T(8,128)} %bitcast.3, s32[1,8]{1,0:T(1,128)} %bitcast.4, s32[1,1]{1,0:T(1,128)S(6)} %copy.9.cut_hbm, bf16[64,1920]{1,0:T(8,128)(2,1)} %qkv_hbm.1, bf16[64,1280]{1,0:T(8,128)(2,1)} %cot_hbm.1, ...), custom_call_target="tpu_custom_call" | custom-call | tf_op jit(solution)/shard_map/pallas_call | solution.py:397
  31.5 0.9 %shard_map.86 = (bf16[64,1280]{1,0:T(8,128)(2,1)}, bf16[64,1920]{1,0:T(8,128)(2,1)}, f32[10,16,640]{2,1,0:T(8,128)}) custom-call(bf16[64,1280]{1,0:T(8,128)(2,1)S(1)} %get-tuple-element.9.emb, bf16[64,1920]{1,0:T(8,128)(2,1)S(1)} %get-tuple-element.10.grad, f32[10,16,640]{2,1,0:T(8,128)S(1)} %get-tuple-element.11.own), custom_call_target="tpu_custom_call" | custom-call | tf_op jit(solution)/shard_map/pallas_call | solution.py:442

commit v4 on v3

--- a/solution.py
+++ b/solution.py
@@ -175,14 +175,6 @@
     loads[2].wait()
     att_grad = dot(cot[...], w[...]).astype(BF16)
     sendg[...] = dot(sel[...], att_grad).reshape(groups, SLOT, hf).astype(BF16)
-    pending_g = []
-    for k in order_k:
-        copy = remote(sendg.at[partner(me, k)], recvg.at[me], sg.at[k], rg.at[k], k)
-        copy.start()
-        pending_g.append(copy)
-    local_g = pltpu.make_async_copy(sendg.at[me], recvg.at[me], loc_sem.at[1])
-    local_g.start()
-
     mark("m06_cot")
     cots[...] = dot(sel[...], cot[...]).reshape(groups, SLOT, width).astype(BF16)
 
@@ -242,31 +234,15 @@
         copy = remote(attall.at[me], attall.at[me], sa.at[k], ra.at[k], k)
         copy.start()
         pending_a.append(copy)
+    pending_g = []
+    for k in order_k:
+        copy = remote(sendg.at[partner(me, k)], recvg.at[me], sg.at[k], rg.at[k], k)
+        copy.start()
+        pending_g.append(copy)
+    local_g = pltpu.make_async_copy(sendg.at[me], recvg.at[me], loc_sem.at[1])
+    local_g.start()
+
     grads[:, :hf] = att
-
-    mark("m09_waitg")
-    local_g.wait()
-    for copy in pending_g:
-        copy.wait_recv()
-    mark("m10_bwd")
-    xg = dot(pack_t[...], flat(recvg[...]), TN).astype(BF16)
-    for h in range(HEADS):
-        gbig[h * pack : (h + 1) * pack, :] = xg * marks[h]
-    prob_grad = dot(values, gbig[...], NT)
-    delta = jnp.sum(probs * prob_grad, axis=0, keepdims=True)
-    score_grad = (probs * (prob_grad - delta) * scale).astype(BF16)
-    grads[:, hf : 2 * hf] = per_head(dot(score_grad, keys, TN))
-    grads[:, 2 * hf : 3 * hf] = dot(score_grad, qbig[...]).astype(BF16)
-    grads[:, 3 * hf :] = dot(probs_b, gbig[...]).astype(BF16)
-
-    backs[...] = dot(pack_t[...], grads[...]).reshape(groups, SLOT, 4 * hf).astype(BF16)
-    pending_b = []
-    for k in order_k:
-        copy = remote(backs.at[partner(me, k)], backr.at[me], sb.at[k], rb.at[k], k)
-        copy.start()
-        pending_b.append(copy)
-    local_b = pltpu.make_async_copy(backs.at[me], backr.at[me], loc_sem.at[3])
-    local_b.start()
 
     mark("m11_waitc")
     local_c.wait()
@@ -322,6 +298,38 @@
             zsend[way, c] = (own[c] + zbuf[way, c].astype(F32)).astype(BF16)
             hop(way, c).start()
 
+    near = (rep >= (reps + 1) // 2).astype(jnp.int32)
+    edge = (rep == 0) | (rep == reps - 1)
+
+    @pl.when(edge)
+    def _():
+        for c in range(chunks):
+            step(near, c)
+
+    mark("m09_waitg")
+    local_g.wait()
+    for copy in pending_g:
+        copy.wait_recv()
+    mark("m10_bwd")
+    xg = dot(pack_t[...], flat(recvg[...]), TN).astype(BF16)
+    for h in range(HEADS):
+        gbig[h * pack : (h + 1) * pack, :] = xg * marks[h]
+    prob_grad = dot(values, gbig[...], NT)
+    delta = jnp.sum(probs * prob_grad, axis=0, keepdims=True)
+    score_grad = (probs * (prob_grad - delta) * scale).astype(BF16)
+    grads[:, hf : 2 * hf] = per_head(dot(score_grad, keys, TN))
+    grads[:, 2 * hf : 3 * hf] = dot(score_grad, qbig[...]).astype(BF16)
+    grads[:, 3 * hf :] = dot(probs_b, gbig[...]).astype(BF16)
+
+    backs[...] = dot(pack_t[...], grads[...]).reshape(groups, SLOT, 4 * hf).astype(BF16)
+    pending_b = []
+    for k in order_k:
+        copy = remote(backs.at[partner(me, k)], backr.at[me], sb.at[k], rb.at[k], k)
+        copy.start()
+        pending_b.append(copy)
+    local_b = pltpu.make_async_copy(backs.at[me], backr.at[me], loc_sem.at[3])
+    local_b.start()
+
     def source_rows():
         mark("m16_waitb")
         local_b.wait()
@@ -333,13 +341,8 @@
         emb[...] = dot(back[:, :hf], w[...], NT).astype(BF16)
         mark("m175")
 
-    near = (rep >= (reps + 1) // 2).astype(jnp.int32)
-    edge = (rep == 0) | (rep == reps - 1)
-
     @pl.when(edge)
     def _():
-        for c in range(chunks):
-            step(near, c)
         source_rows()
         for c in range(chunks):
             step(1 - near, c)

time: 32.6 us -> 32 us (0.982)
  Pallas kernels: 31.1 us -> 30.6 us
    pallas_call x1, Pallas kernels: 30.2 us -> 29.6 us  [local(): pl.pallas_call(functools.partial(kernel, groups, reps), out_shape=(pltpu....]
where the time goes in v4:
time: 32 us; the launch traced here: 31.9 us
  Pallas kernels  30.6 us (96%)
  between operations  1.29 us (4%)
    pallas_call x1, Pallas kernels, local(): pl.pallas_call(functools.partial(kernel, groups, reps), out_shape=(pltpu....  29.6 us
    pallas_call x1, Pallas kernels, local(): pl.pallas_call(write_out, out_shape=(jax.ShapeDtypeStruct((rows, width),...  0.92 us

profile of v4, /device:TPU:0, one launch (start us, length us, event | category | flops | bytes accessed | tf_op | source)
XLA Modules:
  0.0 31.9 jit_solution(4413327931605774672)
XLA Ops:
  1.3 29.6 %shard_map.85 = (bf16[64,1280]{1,0:T(8,128)(2,1)S(1)}, bf16[64,1920]{1,0:T(8,128)(2,1)S(1)}, f32[10,16,640]{2,1,0:T(8,128)S(1)}) custom-call(s32[8,8]{1,0:T(8,128)} %bitcast.3, s32[1,8]{1,0:T(1,128)} %bitcast.4, s32[1,1]{1,0:T(1,128)S(6)} %copy.9.cut_hbm, bf16[64,1920]{1,0:T(8,128)(2,1)} %qkv_hbm.1, bf16[64,1280]{1,0:T(8,128)(2,1)} %cot_hbm.1, ...), custom_call_target="tpu_custom_call" | custom-call | tf_op jit(solution)/shard_map/pallas_call | solution.py:400
  30.9 0.9 %shard_map.86 = (bf16[64,1280]{1,0:T(8,128)(2,1)}, bf16[64,1920]{1,0:T(8,128)(2,1)}, f32[10,16,640]{2,1,0:T(8,128)}) custom-call(bf16[64,1280]{1,0:T(8,128)(2,1)S(1)} %get-tuple-element.9.emb, bf16[64,1920]{1,0:T(8,128)(2,1)S(1)} %get-tuple-element.10.grad, f32[10,16,640]{2,1,0:T(8,128)S(1)} %get-tuple-element.11.own), custom_call_target="tpu_custom_call" | custom-call | tf_op jit(solution)/shard_map/pallas_call | solution.py:445
